TPU v7x, 256 devices: a whole 4x4x8 slice. The times are simulated.
256 devices in a mesh: ctx: 32 (over y, x, core), tp: 8 (over z).
Axes of the slice: x: 4, y: 4, z: 8, core: 2. Of those that a mesh axis runs over, the one named last changes fastest.
Arguments:
- queries: bfloat16 [1, 32768, 4096], P(None, 'ctx', 'tp'), may hold values from -6 to 6
- keys: bfloat16 [1, 32768, 1024], P(None, 'ctx', 'tp'), may hold values from -6 to 6
- values: bfloat16 [1, 32768, 1024], P(None, 'ctx', 'tp'), may hold values from -6 to 6
- gates: int32 [1, 64, 8, 3], P(None, 'ctx', 'tp'), may hold values from 0 to 63, as said below
- out_weight: bfloat16 [4096, 4096], P('tp'), may hold values from -0.09375 to 0.09375
Outputs:
- projected: bfloat16 [1, 32768, 4096], P(None, 'ctx', 'tp')
Inputs may be any that keep to these rules, and one draw needn't show every extreme that they name: `gates`: for each sequence and key-value head, the 6 entries of query blocks 2 c to 2 c + 1 name blocks of 6 different values of (block // 2).
All inputs are finite; a program needn't handle non-finite values.
Results may differ from a plain program's by a relative error of at most 0.015.
Values may be sent and summed in bfloat16 or wider, within the bound.
No kernel may reach another device: no remote copies, remote signals or barrier semaphores. Data moves between devices by JAX's collectives and lax.ppermute only.
A program may use at most 64 MiB of HBM per device.

v0:
```python
import math
import jax
import jax.numpy as jnp
from jax import lax
from jax.sharding import PartitionSpec as P

HD = 128
TOKB = 512
PICKS = 3


def per_device(queries, keys, values, gates, out_weight):
    seq_count, tok_dev, query_width = queries.shape
    kv_heads = keys.shape[2] // HD
    head_group = query_width // HD // kv_heads
    blocks_dev = tok_dev // TOKB
    block_count = seq_count * blocks_dev
    position = lax.axis_index("ctx")
    local_block = jnp.arange(block_count, dtype=jnp.int32) % blocks_dev
    global_block = position * blocks_dev + local_block
    query_blocks = queries.reshape(block_count, TOKB, kv_heads, head_group, HD)
    gate_local = gates.reshape(block_count, kv_heads, PICKS)
    causal = jnp.arange(TOKB)[:, None] >= jnp.arange(TOKB)[None, :]
    score_scale = HD ** (-0.5)
    own_keys = keys.reshape(block_count, TOKB, kv_heads, HD)
    own_values = values.reshape(block_count, TOKB, kv_heads, HD)
    scores = (
        jnp.einsum("nqhgd,nkhd->nhgqk", query_blocks, own_keys, preferred_element_type=jnp.float32)
        * score_scale
    )
    scores = jnp.where(causal, scores, -jnp.inf)
    largest = jnp.max(scores, axis=-1)
    raw_weights = jnp.exp(scores - largest[..., None])
    denominator = jnp.sum(raw_weights, axis=-1)
    weighted = jnp.einsum(
        "nhgqk,nkhd->nhgqd",
        raw_weights.astype(jnp.bfloat16),
        own_values,
        preferred_element_type=jnp.float32,
    )
    key_piece = lax.all_gather(keys, "ctx", axis=1, tiled=True)
    value_piece = lax.all_gather(values, "ctx", axis=1, tiled=True)
    piece_rows = key_piece.shape[1]
    step_rows = math.gcd(piece_rows, TOKB)

    def visit(step_index, carried):
        first_row = step_index * step_rows
        key_sub = lax.dynamic_slice_in_dim(key_piece, step_index * step_rows, step_rows, 1)
        value_sub = lax.dynamic_slice_in_dim(value_piece, step_index * step_rows, step_rows, 1)
        block_index = first_row // TOKB
        chosen = jnp.any(gate_local == block_index, axis=2) & (block_index < global_block)[:, None]

        def update(current):
            run_max, run_total, run_weighted = current
            key_rows = jnp.repeat(key_sub, blocks_dev, axis=0).reshape(
                block_count, step_rows, kv_heads, HD
            )
            value_rows = jnp.repeat(value_sub, blocks_dev, axis=0).reshape(
                block_count, step_rows, kv_heads, HD
            )
            piece_scores = (
                jnp.einsum(
                    "nqhgd,nkhd->nhgqk", query_blocks, key_rows, preferred_element_type=jnp.float32
                )
                * score_scale
            )
            piece_scores = jnp.where(chosen[:, :, None, None, None], piece_scores, -jnp.inf)
            new_max = jnp.maximum(run_max, jnp.max(piece_scores, axis=-1))
            rescale = jnp.exp(run_max - new_max)
            new_weights = jnp.exp(piece_scores - new_max[..., None])
            new_total = run_total * rescale + jnp.sum(new_weights, axis=-1)
            added = jnp.einsum(
                "nhgqk,nkhd->nhgqd",
                new_weights.astype(jnp.bfloat16),
                value_rows,
                preferred_element_type=jnp.float32,
            )
            return (new_max, new_total, run_weighted * rescale[..., None] + added)

        return lax.cond(jnp.any(chosen), update, lambda current: current, carried)

    run_max, run_total, run_weighted = lax.fori_loop(
        0, piece_rows // step_rows, visit, (largest, denominator, weighted)
    )
    attended = (run_weighted / run_total[..., None]).astype(jnp.bfloat16)
    attended = jnp.transpose(attended, (0, 3, 1, 2, 4)).reshape(seq_count, tok_dev, query_width)
    partial_terms = jnp.dot(
        attended.reshape(-1, query_width), out_weight, preferred_element_type=jnp.float32
    )
    partial_terms = partial_terms.astype(jnp.bfloat16).reshape(
        seq_count, tok_dev, out_weight.shape[1]
    )
    return (
        lax.psum_scatter(partial_terms, "tp", scatter_dimension=2, tiled=True)
        .astype(jnp.float32)
        .astype(jnp.bfloat16)
    )


def solution(mesh):
    placed = (
        P(None, "ctx", "tp"),
        P(None, "ctx", "tp"),
        P(None, "ctx", "tp"),
        P(None, "ctx", "tp", None),
        P("tp", None),
    )
    return jax.shard_map(
        per_device, mesh=mesh, in_specs=placed, out_specs=P(None, "ctx", "tp"), check_vma=False
    )
```

profile of v0, /device:TPU:1, one launch (start us, length us, event | category | flops | bytes accessed | tf_op | source)
XLA Modules:
  0.0 382.9 jit_solution(16034697490817509006)
XLA Ops:
  6.5 0.7 all-gather.3.cloned.1.call-update
  7.3 0.7 all-gather.5.cloned.1.call-update
  8.1 1.3 reshape.133
  9.4 1.3 reshape.137
  11.0 2.5 fusion.23
  13.5 1.7 fusion.22
  15.3 2.6 fusion.28
  17.9 54.0 %all-gather.3.cloned.1.call-done = bf16[1,32768,128]{2,1,0:T(8,128)(2,1)} async-done(((bf16[1,1024,128]{2,1,0:T(8,128)(2,1)}), bf16[1,32768,128]{2,1,0:T(8,128)(2,1)}) %all-gather.3.cloned.1.call-update) | async-done | bytes 8388624 | tf_op jit(solution)/shard_map/all_gather | solution.py:41
  71.9 60.0 %all-gather.5.cloned.1.call-done = bf16[1,32768,128]{2,1,0:T(8,128)(2,1)} async-done(((bf16[1,1024,128]{2,1,0:T(8,128)(2,1)}), bf16[1,32768,128]{2,1,0:T(8,128)(2,1)}) %all-gather.5.cloned.1.call-update) | async-done | bytes 8388624 | tf_op jit(solution)/shard_map/all_gather | solution.py:42
  131.9 102.1 %while.20 = (s32[]{:T(128)}, f32[2,1,4,512]{3,2,0,1:T(4,128)S(1)}, f32[2,1,4,512]{3,2,0,1:T(4,128)S(1)}, f32[2,1,4,512,128]{4,3,2,0,1:T(8,128)S(1)}, s32[2,1,3]{...) while((s32[]{:T(128)}, f32[2,1,4,512]{3,2,0,1:T(4,128)S(1)}, ...), condition=%wide.region_9.10_spmd.clone, body=%wide.region_2.9_spmd.clone.sunk | while | flops 1097871360 | bytes 31457836 | solution.py:82
  132.1 0.7 and_reduce_fusion.2
  133.5 0.7 and_reduce_fusion.2
  134.8 7.5 %conditional.3 = ((f32[2,1,4,512]{3,2,0,1:T(4,128)S(1)}, f32[2,1,4,512]{3,2,0,1:T(4,128)S(1)}, f32[2,1,4,512,128]{4,3,2,0,1:T(8,128)S(1)})) conditional(s32[]{:T(128)} %convert_element_type.48, (f32[2,1,4,512]{3,2,0,1:T(4,128)S(1)}, f32[2,1,4,512]{3,2,0,1:T(4,128)S(1)}, f32[2,1,4,512,128]{4,3,2,0,1:T(8,128)S(1)}) %tuple.65, (s32[]{:T(128)}, ...), branch_computations={%region_5.5_spmd, %region_6.8_spmd} | conditional | flops 1097871360 | bytes 31457362 | solution.py:80
  134.9 1.0 dynamic-slice_bitcast_fusion
  135.9 1.3 bitcast_reduce_fusion
  137.2 3.4 bitcast_add_fusion
  140.6 1.7 fusion.4
  142.5 0.7 and_reduce_fusion.2
  144.0 0.7 and_reduce_fusion.2
  145.5 0.7 and_reduce_fusion.2
  147.0 0.7 and_reduce_fusion.2
  148.5 0.7 and_reduce_fusion.2
  149.9 0.7 and_reduce_fusion.2
  151.4 0.7 and_reduce_fusion.2
  152.9 0.7 and_reduce_fusion.2
  154.4 0.7 and_reduce_fusion.2
  155.8 0.7 and_reduce_fusion.2
  157.3 0.7 and_reduce_fusion.2
  158.8 0.7 and_reduce_fusion.2
  160.3 0.7 and_reduce_fusion.2
  161.8 0.7 and_reduce_fusion.2
  163.2 0.7 and_reduce_fusion.2
  164.7 0.7 and_reduce_fusion.2
  166.2 0.7 and_reduce_fusion.2
  167.7 0.7 and_reduce_fusion.2
  169.2 0.7 and_reduce_fusion.2
  170.6 0.7 and_reduce_fusion.2
  172.1 0.7 and_reduce_fusion.2
  173.6 0.7 and_reduce_fusion.2
  175.1 0.7 and_reduce_fusion.2
  176.6 0.7 and_reduce_fusion.2
  178.0 0.7 and_reduce_fusion.2
  189.9 0.7 and_reduce_fusion.2
  218.0 0.7 and_reduce_fusion.2
  234.1 0.7 fusion.35
  234.8 0.8 copy.15
  235.6 8.9 %convert_bitcast_fusion = bf16[1,1024,4096]{2,1,0:T(8,128)(2,1)} fusion(bf16[512,4096]{1,0:T(8,128)(2,1)} %param.13, bf16[128,8,4,128]{3,2,1,0:T(4,128)(2,1)S(1)} %bitcast.116), kind=kOutput, calls=%fused_computation.31 | convolution fusion | flops 4299161600 | bytes 13631488 | tf_op jit(solution)/shard_map/dot_general | solution.py:87
  244.6 131.8 %reduce-scatter.2.cloned.1.call-done = bf16[1,1024,512]{2,1,0:T(8,128)(2,1)} async-done(((bf16[1,1024,4096]{2,1,0:T(8,128)(2,1)}), bf16[1,1024,512]{2,1,0:T(8,128)(2,1)}) %reduce-scatter.2.cloned.1.call-update) | async-done | bytes 1048592 | tf_op jit(solution)/shard_map/reduce_scatter | solution.py:94
  (240 shorter events, 32.8 us)
Async XLA Ops:
  6.5 65.4 %all-gather.3.cloned.1.call-start = ((), (), s32[]{:S(2)}) async-start(), calls=%async_computation.1 | async-start | bytes 8650752 | tf_op jit(solution)/shard_map/all_gather | solution.py:41
  7.3 124.7 %all-gather.5.cloned.1.call-start = ((), (), s32[]{:S(2)}) async-start(), calls=%async_computation.2 | async-start | bytes 8650752 | tf_op jit(solution)/shard_map/all_gather | solution.py:42
  8.0 368.4 %reduce-scatter.2.cloned.1.call-start = ((), (), s32[]{:S(2)}) async-start(), calls=%async_computation.3 | async-start | bytes 9437184 | tf_op jit(solution)/shard_map/reduce_scatter | solution.py:94
  11.0 4.3 %copy-start = (bf16[1,1024,128]{2,1,0:T(8,128)(2,1)S(1)}, bf16[1,1024,128]{2,1,0:T(8,128)(2,1)}, u32[]{:S(2)}) copy-start(bf16[1,1024,128]{2,1,0:T(8,128)(2,1)} %param.11) | copy-start | bytes 786436
  15.3 116.6 %copy-start.1 = (s32[1,2,1,3]{3,2,1,0:T(1,128)S(1)}, s32[1,2,1,3]{3,2,1,0:T(1,128)}, u32[]{:S(2)}) copy-start(s32[1,2,1,3]{3,2,1,0:T(1,128)} %param.12) | copy-start | bytes 76
Sparse Core Ops, SparseCore 0:
  9.9 61.9 all-gather.2
  74.5 57.4 all-gather.4
  244.7 131.6 reduce-scatter.1
where the time goes:
time: 384 us; the launch traced here: 383 us
  waiting for transfers between devices  247 us (64%)
  other arithmetic  55.4 us (14%)
  loops' own time  43.6 us (11%)
  matrix products  18.7 us (5%)
  between operations  13.2 us (3%)
  local copies, waits for them, and re-layouts  4.65 us (1%)
    reduce_scatter x1, waiting for transfers between devices, per_device(): lax.psum_scatter(partial_terms, 'tp', scatter_dimension=2, tiled=True)  132 us
    all_gather x1, waiting for transfers between devices, per_device(): value_piece = lax.all_gather(values, 'ctx', axis=1, tiled=True)  60 us
    all_gather x1, waiting for transfers between devices, per_device(): key_piece = lax.all_gather(keys, 'ctx', axis=1, tiled=True)  54 us
    reduce_or x64, other arithmetic, visit(): return lax.cond(jnp.any(chosen), update, lambda current: current, carried)  42.8 us
    another operation x1, loops' own time, per_device(): lax.fori_loop(0, piece_rows // step_rows, visit, (largest, denominator, w...  42.8 us
    dot_general x1, matrix products, per_device(): jnp.dot(attended.reshape(-1, query_width), out_weight, preferred_element_...  8.92 us
    reduce_or x64, other arithmetic, visit(): jnp.any(gate_local == block_index, axis=2)  7.78 us
  transfers between devices with their start and end apart: 3, of which 3 were waited for; matrix products, arithmetic and copies ran while one was open for 3% of the time, Pallas kernels for 0%

commit v1 on v0

--- a/solution.py
+++ b/solution.py
@@ -39,7 +39,9 @@
         preferred_element_type=jnp.float32,
     )
     key_piece = lax.all_gather(keys, "ctx", axis=1, tiled=True)
-    value_piece = lax.all_gather(values, "ctx", axis=1, tiled=True)
+    value_piece = jnp.concatenate(
+        lax.all_to_all(jnp.stack([values] * lax.axis_size("ctx")), "ctx", 0, 0), axis=1
+    )
     piece_rows = key_piece.shape[1]
     step_rows = math.gcd(piece_rows, TOKB)
 

time: 384 us -> 396 us (1.031)
  starting transfers between devices: 0.08 us -> 8.81 us
    all_to_all x0 -> x1, waiting for transfers between devices: none -> 104 us  [per_device(): lax.all_to_all(jnp.stack([values] * lax.axis_size('ctx')), 'ctx', 0, 0)]
    all_gather x1 -> x0, waiting for transfers between devices: 60 us -> none  [per_device(): value_piece = lax.all_gather(values, 'ctx', axis=1, tiled=True)]
    all_gather x1, waiting for transfers between devices: 54 us -> 7.48 us  [per_device(): key_piece = lax.all_gather(keys, 'ctx', axis=1, tiled=True)]
    all_to_all x0 -> x1, starting transfers between devices: none -> 8.76 us  [per_device(): lax.all_to_all(jnp.stack([values] * lax.axis_size('ctx')), 'ctx', 0, 0)]
    another operation x2 -> x3, local copies, waits for them, and re-layouts: 2.34 us -> 7.34 us  [the longest x1 6.06 us: per_device(): jnp.stack([values] * lax.axis_size('ctx'))]
where the time goes in v1:
time: 396 us; the launch traced here: 395 us
  waiting for transfers between devices  247 us (62%)
  other arithmetic  54.3 us (14%)
  loops' own time  44.6 us (11%)
  matrix products  17.9 us (5%)
  between operations  13.5 us (3%)
  starting transfers between devices  8.81 us (2%)
  local copies, waits for them, and re-layouts  8.6 us (2%)
    reduce_scatter x1, waiting for transfers between devices, per_device(): lax.psum_scatter(partial_terms, 'tp', scatter_dimension=2, tiled=True)  135 us
    all_to_all x1, waiting for transfers between devices, per_device(): lax.all_to_all(jnp.stack([values] * lax.axis_size('ctx')), 'ctx', 0, 0)  104 us
    another operation x1, loops' own time, per_device(): lax.fori_loop(0, piece_rows // step_rows, visit, (largest, denominator, w...  43.8 us
    reduce_or x64, other arithmetic, visit(): return lax.cond(jnp.any(chosen), update, lambda current: current, carried)  41.7 us
    dot_general x1, matrix products, per_device(): jnp.dot(attended.reshape(-1, query_width), out_weight, preferred_element_...  8.91 us
    all_to_all x1, starting transfers between devices, per_device(): lax.all_to_all(jnp.stack([values] * lax.axis_size('ctx')), 'ctx', 0, 0)  8.76 us
  transfers between devices with their start and end apart: 3, of which 3 were waited for; matrix products, arithmetic and copies ran while one was open for 3% of the time, Pallas kernels for 0%

profile of v1, /device:TPU:1, one launch (start us, length us, event | category | flops | bytes accessed | tf_op | source)
XLA Modules:
  0.0 394.9 jit_solution(6888350748640488151)
XLA Ops:
  6.5 0.7 all-gather.2.cloned.1.call-update
  7.3 6.1 %stack.2 = bf16[32,1,1024,128]{3,2,1,0:T(8,128)(2,1)} broadcast(bf16[1024,128]{1,0:T(8,128)(2,1)} %bitcast.121), dimensions={2,3} | broadcast | bytes 8650752 | tf_op jit(solution)/shard_map/stack | solution.py:43
  13.3 8.8 %all-to-all-start = ((bf16[32,1,1024,128]{3,2,1,0:T(8,128)(2,1)}), bf16[32,1,1024,128]{3,2,1,0:T(8,128)(2,1)}, u32[]{:S(2)}, u32[]{:S(2)}) async-start(bf16[32,1,1024,128]{3,2,1,0:T(8,128)(2,1)} %stack.2), calls=%async_computation | async-start | bytes 16777216 | tf_op jit(solution)/shard_map/all_to_all | solution.py:43
  23.0 1.8 fusion.23
  24.8 1.7 fusion.22
  26.6 2.5 fusion.28
  29.1 104.0 %all-to-all-done = bf16[32,1,1024,128]{3,2,1,0:T(8,128)(2,1)} async-done(((bf16[32,1,1024,128]{3,2,1,0:T(8,128)(2,1)}), bf16[32,1,1024,128]{3,2,1,0:T(8,128)(2,1)}, u32[]{:S(2)}, u32[]{:S(2)}) %all-to-all-start) | async-done | bytes 8388640 | tf_op jit(solution)/shard_map/all_to_all | solution.py:43
  133.1 7.5 %all-gather.2.cloned.1.call-done = bf16[1,32768,128]{2,1,0:T(8,128)(2,1)} async-done(((bf16[1,1024,128]{2,1,0:T(8,128)(2,1)}), bf16[1,32768,128]{2,1,0:T(8,128)(2,1)}) %all-gather.2.cloned.1.call-update) | async-done | bytes 8388624 | tf_op jit(solution)/shard_map/all_gather | solution.py:41
  140.6 102.0 %while.20 = (s32[]{:T(128)}, f32[2,1,4,512]{3,2,0,1:T(4,128)S(1)}, f32[2,1,4,512]{3,2,0,1:T(4,128)S(1)}, f32[2,1,4,512,128]{4,3,2,0,1:T(8,128)S(1)}, s32[2,1,3]{...) while((s32[]{:T(128)}, f32[2,1,4,512]{3,2,0,1:T(4,128)S(1)}, ...), condition=%wide.region_9.10_spmd.clone, body=%wide.region_2.9_spmd.clone.sunk | while | flops 1097871360 | bytes 31457836 | solution.py:84
  143.5 7.5 %conditional.3 = ((f32[2,1,4,512]{3,2,0,1:T(4,128)S(1)}, f32[2,1,4,512]{3,2,0,1:T(4,128)S(1)}, f32[2,1,4,512,128]{4,3,2,0,1:T(8,128)S(1)})) conditional(s32[]{:T(128)} %convert_element_type.48, (f32[2,1,4,512]{3,2,0,1:T(4,128)S(1)}, f32[2,1,4,512]{3,2,0,1:T(4,128)S(1)}, f32[2,1,4,512,128]{4,3,2,0,1:T(8,128)S(1)}) %tuple.66, (s32[]{:T(128)}, ...), branch_computations={%region_5.5_spmd, %region_6.8_spmd} | conditional | flops 1097871360 | bytes 31457362 | solution.py:82
  143.5 1.0 dynamic-slice_bitcast_fusion
  144.5 1.3 bitcast_reduce_fusion
  145.8 3.4 bitcast_add_fusion
  149.2 1.7 fusion.4
  152.7 0.7 and_reduce_fusion.2
  154.1 0.7 and_reduce_fusion.2
  155.6 0.7 and_reduce_fusion.2
  157.1 0.7 and_reduce_fusion.2
  158.6 0.7 and_reduce_fusion.2
  160.0 0.7 and_reduce_fusion.2
  167.4 0.7 and_reduce_fusion.2
  168.9 0.7 and_reduce_fusion.2
  170.4 0.7 and_reduce_fusion.2
  171.9 0.7 and_reduce_fusion.2
  173.3 0.7 and_reduce_fusion.2
  174.8 0.7 and_reduce_fusion.2
  180.7 0.7 and_reduce_fusion.2
  182.2 0.7 and_reduce_fusion.2
  183.7 0.7 and_reduce_fusion.2
  185.1 0.7 and_reduce_fusion.2
  186.6 0.7 and_reduce_fusion.2
  188.1 0.7 and_reduce_fusion.2
  195.5 0.7 and_reduce_fusion.2
  197.0 0.7 and_reduce_fusion.2
  198.4 0.7 and_reduce_fusion.2
  199.9 0.7 and_reduce_fusion.2
  201.4 0.7 and_reduce_fusion.2
  202.9 0.7 and_reduce_fusion.2
  208.8 0.7 and_reduce_fusion.2
  210.2 0.7 and_reduce_fusion.2
  211.7 0.7 and_reduce_fusion.2
  213.2 0.7 and_reduce_fusion.2
  214.7 0.7 and_reduce_fusion.2
  216.2 0.7 and_reduce_fusion.2
  242.6 0.7 fusion.35
  243.3 0.8 copy.21
  244.1 8.9 %convert_bitcast_fusion = bf16[1,1024,4096]{2,1,0:T(8,128)(2,1)} fusion(bf16[512,4096]{1,0:T(8,128)(2,1)} %param.13, bf16[128,8,4,128]{3,2,1,0:T(4,128)(2,1)S(1)} %bitcast.118), kind=kOutput, calls=%fused_computation.31 | convolution fusion | flops 4299161600 | bytes 13631488 | tf_op jit(solution)/shard_map/dot_general | solution.py:89
  253.1 135.0 %reduce-scatter.2.cloned.1.call-done = bf16[1,1024,512]{2,1,0:T(8,128)(2,1)} async-done(((bf16[1,1024,4096]{2,1,0:T(8,128)(2,1)}), bf16[1,1024,512]{2,1,0:T(8,128)(2,1)}) %reduce-scatter.2.cloned.1.call-update) | async-done | bytes 1048592 | tf_op jit(solution)/shard_map/reduce_scatter | solution.py:96
  (244 shorter events, 32.1 us)
Async XLA Ops:
  6.5 134.0 %all-gather.2.cloned.1.call-start = ((), (), s32[]{:S(2)}) async-start(), calls=%async_computation.2 | async-start | bytes 8650752 | tf_op jit(solution)/shard_map/all_gather | solution.py:41
  13.3 8.8 %copy-start = (bf16[1,1024,512]{2,1,0:T(8,128)(2,1)S(1)}, bf16[1,1024,512]{2,1,0:T(8,128)(2,1)}, u32[]{:S(2)}) copy-start(bf16[1,1024,512]{2,1,0:T(8,128)(2,1)} %param.9) | copy-start | bytes 3145732
  13.3 9.7 %copy-start.1 = (bf16[1,1024,128]{2,1,0:T(8,128)(2,1)S(1)}, bf16[1,1024,128]{2,1,0:T(8,128)(2,1)}, u32[]{:S(2)}) copy-start(bf16[1,1024,128]{2,1,0:T(8,128)(2,1)} %param.10) | copy-start | bytes 786436
  13.3 119.8 %all-to-all-start = ((bf16[32,1,1024,128]{3,2,1,0:T(8,128)(2,1)}), bf16[32,1,1024,128]{3,2,1,0:T(8,128)(2,1)}, u32[]{:S(2)}, u32[]{:S(2)}) async-start(bf16[32,1,1024,128]{3,2,1,0:T(8,128)(2,1)} %stack.2), calls=%async_computation | async-start | bytes 16777216 | tf_op jit(solution)/shard_map/all_to_all | solution.py:43
  22.1 366.0 %reduce-scatter.2.cloned.1.call-start = ((), (), s32[]{:S(2)}) async-start(), calls=%async_computation.3 | async-start | bytes 9437184 | tf_op jit(solution)/shard_map/reduce_scatter | solution.py:96
  23.0 3.6 copy-start.2
  26.5 114.0 %copy-start.3 = (s32[1,2,1,3]{3,2,1,0:T(1,128)S(1)}, s32[1,2,1,3]{3,2,1,0:T(1,128)}, u32[]{:S(2)}) copy-start(s32[1,2,1,3]{3,2,1,0:T(1,128)} %param.12) | copy-start | bytes 76
Sparse Core Ops, SparseCore 0:
  9.9 130.6 all-gather.1
  253.2 134.8 reduce-scatter.1

commit v2 on v0

--- a/solution.py
+++ b/solution.py
@@ -38,8 +38,11 @@
         own_values,
         preferred_element_type=jnp.float32,
     )
-    key_piece = lax.all_gather(keys, "ctx", axis=1, tiled=True)
-    value_piece = lax.all_gather(values, "ctx", axis=1, tiled=True)
+    key_piece, value_piece = jnp.split(
+        lax.all_gather(jnp.concatenate([keys, values], axis=0), "ctx", axis=1, tiled=True),
+        [keys.shape[0]],
+        axis=0,
+    )
     piece_rows = key_piece.shape[1]
     step_rows = math.gcd(piece_rows, TOKB)
 

time: 384 us -> 360 us (0.938)
  waiting for transfers between devices: 247 us -> 205 us
  local copies, waits for them, and re-layouts: 4.65 us -> 15.9 us
  other arithmetic: 55.4 us -> 60.2 us
    all_gather x2 -> x1, waiting for transfers between devices: 114 us -> 73.5 us  [per_device(): lax.all_gather(jnp.concatenate([keys, values], axis=0), 'ctx', axis=1, ti...]
    split x0 -> x1, local copies, waits for them, and re-layouts: none -> 11.3 us  [per_device(): jnp.split(lax.all_gather(jnp.concatenate([keys, values], axis=0), 'ctx',...]
  transfers between devices with their start and end apart: 3 -> 2, of which waited for: 3 -> 2; matrix products, arithmetic and copies ran while one was open for 3% -> 3% of each run, Pallas kernels for 0% -> 0%
where the time goes in v2:
time: 360 us; the launch traced here: 359 us
  waiting for transfers between devices  205 us (57%)
  other arithmetic  60.2 us (17%)
  loops' own time  45.5 us (13%)
  matrix products  18.6 us (5%)
  local copies, waits for them, and re-layouts  15.9 us (4%)
  between operations  13.5 us (4%)
    reduce_scatter x1, waiting for transfers between devices, per_device(): lax.psum_scatter(partial_terms, 'tp', scatter_dimension=2, tiled=True)  132 us
    all_gather x1, waiting for transfers between devices, per_device(): lax.all_gather(jnp.concatenate([keys, values], axis=0), 'ctx', axis=1, ti...  73.5 us
    reduce_or x64, other arithmetic, visit(): return lax.cond(jnp.any(chosen), update, lambda current: current, carried)  45.8 us
    another operation x1, loops' own time, per_device(): lax.fori_loop(0, piece_rows // step_rows, visit, (largest, denominator, w...  44.5 us
    split x1, local copies, waits for them, and re-layouts, per_device(): jnp.split(lax.all_gather(jnp.concatenate([keys, values], axis=0), 'ctx',...  11.3 us
    dot_general x1, matrix products, per_device(): jnp.dot(attended.reshape(-1, query_width), out_weight, preferred_element_...  8.91 us
    reduce_or x64, other arithmetic, visit(): jnp.any(gate_local == block_index, axis=2)  7.78 us
  transfers between devices with their start and end apart: 2, of which 2 were waited for; matrix products, arithmetic and copies ran while one was open for 3% of the time, Pallas kernels for 0%

profile of v2, /device:TPU:1, one launch (start us, length us, event | category | flops | bytes accessed | tf_op | source)
XLA Modules:
  0.0 359.2 jit_solution(11223270412629816383)
XLA Ops:
  6.5 1.9 pad_maximum_fusion
  8.5 1.3 reshape.137
  9.8 1.3 reshape.133
  11.4 2.5 fusion.23
  14.0 1.7 fusion.22
  15.7 2.5 fusion.28
  18.2 73.5 %all-gather.2.cloned.1.call-done = bf16[2,32768,128]{2,1,0:T(8,128)(2,1)} async-done(((bf16[2,1024,128]{2,1,0:T(8,128)(2,1)}), bf16[2,32768,128]{2,1,0:T(8,128)(2,1)}) %all-gather.2.cloned.1.call-update) | async-done | bytes 16777232 | tf_op jit(solution)/shard_map/all_gather | solution.py:42
  91.7 11.3 %fusion.38 = (bf16[1,32768,128]{2,1,0:T(8,128)(2,1)}, bf16[1,32768,128]{2,1,0:T(8,128)(2,1)}) fusion(bf16[2,32768,128]{2,1,0:T(8,128)(2,1)} %all-gather.2.cloned.1.call-done), kind=kLoop, calls=%fused_computation.50 | loop fusion | bytes 33554432 | tf_op jit(solution)/shard_map/split | solution.py:41
  103.0 107.1 %while.20 = (s32[]{:T(128)}, f32[2,1,4,512]{3,2,0,1:T(4,128)S(1)}, f32[2,1,4,512]{3,2,0,1:T(4,128)S(1)}, f32[2,1,4,512,128]{4,3,2,0,1:T(8,128)S(1)}, s32[2,1,3]{...) while((s32[]{:T(128)}, f32[2,1,4,512]{3,2,0,1:T(4,128)S(1)}, ...), condition=%wide.region_9.10_spmd.clone, body=%wide.region_2.9_spmd.clone.sunk | while | flops 1097871360 | bytes 31457836 | solution.py:85
  103.1 0.7 and_reduce_fusion.2
  104.7 0.7 and_reduce_fusion.2
  106.0 7.5 %conditional.3 = ((f32[2,1,4,512]{3,2,0,1:T(4,128)S(1)}, f32[2,1,4,512]{3,2,0,1:T(4,128)S(1)}, f32[2,1,4,512,128]{4,3,2,0,1:T(8,128)S(1)})) conditional(s32[]{:T(128)} %convert_element_type.48, (f32[2,1,4,512]{3,2,0,1:T(4,128)S(1)}, f32[2,1,4,512]{3,2,0,1:T(4,128)S(1)}, f32[2,1,4,512,128]{4,3,2,0,1:T(8,128)S(1)}) %tuple.66, (s32[]{:T(128)}, ...), branch_computations={%region_5.5_spmd, %region_6.8_spmd} | conditional | flops 1097871360 | bytes 31457362 | solution.py:83
  106.1 1.0 dynamic-slice_bitcast_fusion
  107.1 1.3 bitcast_reduce_fusion
  108.4 1.7 fusion.4
  110.1 3.4 bitcast_add_fusion
  113.8 0.7 and_reduce_fusion.2
  115.3 0.7 and_reduce_fusion.2
  116.9 0.7 and_reduce_fusion.2
  118.4 0.7 and_reduce_fusion.2
  120.0 0.7 and_reduce_fusion.2
  121.5 0.7 and_reduce_fusion.2
  123.1 0.7 and_reduce_fusion.2
  124.7 0.7 and_reduce_fusion.2
  126.2 0.7 and_reduce_fusion.2
  127.8 0.7 and_reduce_fusion.2
  129.3 0.7 and_reduce_fusion.2
  130.9 0.7 and_reduce_fusion.2
  132.4 0.7 and_reduce_fusion.2
  134.0 0.7 and_reduce_fusion.2
  135.5 0.7 and_reduce_fusion.2
  137.1 0.7 and_reduce_fusion.2
  138.7 0.7 and_reduce_fusion.2
  140.2 0.7 and_reduce_fusion.2
  141.8 0.7 and_reduce_fusion.2
  143.3 0.7 and_reduce_fusion.2
  144.9 0.7 and_reduce_fusion.2
  148.0 0.7 and_reduce_fusion.2
  171.3 0.7 and_reduce_fusion.2
  174.4 0.7 and_reduce_fusion.2
  177.5 0.7 and_reduce_fusion.2
  200.9 0.7 and_reduce_fusion.2
  204.0 0.7 and_reduce_fusion.2
  207.1 0.7 and_reduce_fusion.2
  210.1 0.7 fusion.35
  210.8 0.8 copy.15
  211.6 8.9 %convert_bitcast_fusion = bf16[1,1024,4096]{2,1,0:T(8,128)(2,1)} fusion(bf16[512,4096]{1,0:T(8,128)(2,1)} %param.13, bf16[128,8,4,128]{3,2,1,0:T(4,128)(2,1)S(1)} %bitcast.115), kind=kOutput, calls=%fused_computation.31 | convolution fusion | flops 4299161600 | bytes 13631488 | tf_op jit(solution)/shard_map/dot_general | solution.py:90
  220.6 131.8 %reduce-scatter.2.cloned.1.call-done = bf16[1,1024,512]{2,1,0:T(8,128)(2,1)} async-done(((bf16[1,1024,4096]{2,1,0:T(8,128)(2,1)}), bf16[1,1024,512]{2,1,0:T(8,128)(2,1)}) %reduce-scatter.2.cloned.1.call-update) | async-done | bytes 1048592 | tf_op jit(solution)/shard_map/reduce_scatter | solution.py:97
  (239 shorter events, 34.0 us)
Async XLA Ops:
  6.5 85.2 %all-gather.2.cloned.1.call-start = ((), (), s32[]{:S(2)}) async-start(), calls=%async_computation.1 | async-start | bytes 17301504 | tf_op jit(solution)/shard_map/all_gather | solution.py:42
  8.4 343.9 %reduce-scatter.2.cloned.1.call-start = ((), (), s32[]{:S(2)}) async-start(), calls=%async_computation.2 | async-start | bytes 9437184 | tf_op jit(solution)/shard_map/reduce_scatter | solution.py:97
  11.4 4.3 %copy-start = (bf16[1,1024,128]{2,1,0:T(8,128)(2,1)S(1)}, bf16[1,1024,128]{2,1,0:T(8,128)(2,1)}, u32[]{:S(2)}) copy-start(bf16[1,1024,128]{2,1,0:T(8,128)(2,1)} %param.11) | copy-start | bytes 786436
  18.2 84.8 %copy-start.1 = (s32[1,2,1,3]{3,2,1,0:T(1,128)S(1)}, s32[1,2,1,3]{3,2,1,0:T(1,128)}, u32[]{:S(2)}) copy-start(s32[1,2,1,3]{3,2,1,0:T(1,128)} %param.12) | copy-start | bytes 76
Sparse Core Ops, SparseCore 0:
  9.9 81.7 all-gather.1
  220.7 131.6 reduce-scatter.1
